TPU v7x, 128 devices: a whole 4x4x4 slice. The times are simulated.
128 devices in a mesh: req: 16 (over y, x), seq: 8 (over z, core).
Axes of the slice: x: 4, y: 4, z: 4, core: 2. Of those that a mesh axis runs over, the one named last changes fastest.
Arguments:
- qkv_proj: bfloat16 [16, 1024, 4096], P('req', 'seq'), may hold values from -6 to 6
- gate_proj: bfloat16 [16, 1024, 2048], P('req', 'seq'), may hold values from -6 to 6
- residual: bfloat16 [16, 1024, 2048], P('req', 'seq'), may hold values from -6 to 6
- log_decay: float32 [16, 1024, 8], P('req', 'seq'), may hold values from -1 to 0, as said below
- beta_logit: bfloat16 [16, 1024, 8], P('req', 'seq'), may hold values from -6 to 6
- lengths: int32 [16], replicated, may hold values from 1 to 1024, 8192 in all
- slot_request: int32 [16], replicated, may hold values from 0 to 15, each once
- conv_weight: float32 [4, 4096], replicated, may hold values from -3 to 3
- norm_gain: float32 [256], replicated, may hold values from 0.1 to 1.9
- out_weight: bfloat16 [2048, 2048], P(('req', 'seq')), may hold values from -0.125 to 0.125
- mlp_gain: float32 [2048], replicated, may hold values from 0.1 to 1.9
- w_gate: bfloat16 [2048, 5632], P('req', 'seq'), may hold values from -0.125 to 0.125
- w_up: bfloat16 [2048, 5632], P('req', 'seq'), may hold values from -0.125 to 0.125
- w_down: bfloat16 [5632, 2048], P('seq', 'req'), may hold values from -0.078125 to 0.078125
Outputs:
- hidden_out: bfloat16 [16, 1024, 2048], P('req', 'seq')
- final_state: float32 [16, 8, 128, 256], P('req', 'seq')
- conv_edge: bfloat16 [16, 3, 4096], P('req', None, 'seq')
Inputs may be any that keep to these rules, and one draw needn't show every extreme that they name: Slot s of the req axis holds request slot_request[s]. The 16 lengths sum to 8192, and the longest is exactly 1024. `log_decay`: every entry is negative.
All inputs are finite; a program needn't handle non-finite values.
Results may differ from a plain program's by a relative error of at most 0.014.
Values may be sent and summed in bfloat16 or wider, within the bound.
A program may use at most 128 MiB of HBM per device.

v0:
```python
import jax
import jax.numpy as jnp
from jax import lax
from jax.sharding import PartitionSpec as P

LOCAL_HEADS = 8
DK = 128
DV = 256
CONV = 4
BLOCK = 64
HK = 1024


EPS_NORM = 1e-05
EPS_UNIT = 1e-06
HIGHEST = lax.Precision.HIGHEST


def shifted(value, axis, steps):
    count = lax.axis_size(axis)
    initial, last = (max(0, -steps), min(count, count - steps))
    return lax.ppermute(value, axis, [(source, source + steps) for source in range(initial, last)])


def unit_norm(vector):
    return vector * lax.rsqrt(jnp.sum(vector * vector, axis=-1, keepdims=True) + EPS_UNIT)


def to_blocks(tensor, block_len):
    length = tensor.shape[0]
    grouped = tensor.reshape((length // block_len, block_len) + tensor.shape[1:])
    return jnp.moveaxis(grouped, 2, 0)


def block_tables(query_vec, key_vecs, beta_gate, decay_log, block_len):
    query_b = to_blocks(query_vec, block_len)
    keys_b = to_blocks(key_vecs, block_len)
    beta_b = to_blocks(beta_gate, block_len)
    cumulative = jnp.cumsum(to_blocks(decay_log, block_len), axis=-1)
    spread = cumulative[..., :, None] - cumulative[..., None, :]
    lower_full = jnp.tril(jnp.ones((block_len, block_len), jnp.float32))
    lower_strict = jnp.tril(jnp.ones((block_len, block_len), jnp.float32), -1)
    within = jnp.exp(jnp.where(lower_full > 0, spread, 0.0)) * lower_full
    key_inner = jnp.einsum("hnik,hnjk->hnij", keys_b, keys_b, precision=HIGHEST)
    couple = beta_b[..., :, None] * within * lower_strict * key_inner
    identity = jnp.broadcast_to(jnp.eye(block_len, dtype=jnp.float32), couple.shape)
    inverse = lax.linalg.triangular_solve(
        identity + couple, identity, left_side=True, lower=True, unit_diagonal=True
    )
    growth = jnp.exp(cumulative)
    weighted_keys = jnp.einsum(
        "hnij,hnjk->hnik", inverse, (beta_b * growth)[..., None] * keys_b, precision=HIGHEST
    )
    query_keys = jnp.einsum("hnik,hnjk->hnij", query_b, keys_b, precision=HIGHEST) * within
    grown_query = growth[..., None] * query_b
    keys_to_end = jnp.exp(cumulative[..., -1:] - cumulative)[..., None] * keys_b
    end_growth = growth[..., -1]
    return (inverse, beta_b, (weighted_keys, query_keys, grown_query, keys_to_end, end_growth))


def solve_values(inverse, beta_b, values_b):
    return jnp.einsum("hnij,hnjx->hnix", inverse, beta_b[..., None] * values_b, precision=HIGHEST)


def run_blocks(initial, solved, tables):
    weighted_keys, query_keys, grown_query, keys_to_end, end_growth = tables
    sequence = tuple(
        (
            jnp.moveaxis(tensor, 1, 0)
            for tensor in (solved, weighted_keys, query_keys, grown_query, keys_to_end, end_growth)
        )
    )

    def advance(running, inputs_now):
        solved_now, weighted_now, inner_now, query_now, keys_now, growth_now = inputs_now
        corrected = solved_now - jnp.einsum(
            "hck,hkx->hcx", weighted_now, running, precision=HIGHEST
        )
        output_now = jnp.einsum("hck,hkx->hcx", query_now, running, precision=HIGHEST) + jnp.einsum(
            "hcd,hdx->hcx", inner_now, corrected, precision=HIGHEST
        )
        running = growth_now[:, None, None] * running + jnp.einsum(
            "hck,hcx->hkx", keys_now, corrected, precision=HIGHEST
        )
        return (running, output_now)

    return lax.scan(advance, initial, sequence)


def local(
    qkv_proj,
    gate_proj,
    residual,
    log_decay,
    beta_logit,
    lengths,
    slot_request,
    conv_weight,
    norm_gain,
    out_weight,
    mlp_gain,
    w_gate,
    w_up,
    w_down,
):
    seq_index = lax.axis_index("seq")
    req_index = lax.axis_index("req")
    seq_size = lax.axis_size("seq")
    piece_len = qkv_proj.shape[1]
    channels = qkv_proj.shape[2]
    request_ids = jnp.arange(slot_request.shape[0], dtype=jnp.int32)
    request = jnp.sum(jnp.where(request_ids == req_index, slot_request, 0))
    length = jnp.sum(jnp.where(request_ids == request, lengths, 0))
    position = seq_index * piece_len + jnp.arange(piece_len, dtype=jnp.int32)
    live_mask = position < length
    tokens = qkv_proj[0]
    rim_rows = shifted(tokens[piece_len - (CONV - 1) :], "seq", 1)
    extended = jnp.concatenate([rim_rows, tokens], axis=0)
    convolved = jnp.zeros((piece_len, channels), jnp.float32)
    for offset in range(CONV):
        convolved = convolved + conv_weight[offset] * extended[offset : offset + piece_len].astype(
            jnp.float32
        )
    activated = jax.nn.silu(convolved)
    query_vec = unit_norm(activated[:, :HK].reshape(piece_len, LOCAL_HEADS, DK)) * DK ** (-0.5)
    key_vecs = unit_norm(activated[:, HK : 2 * HK].reshape(piece_len, LOCAL_HEADS, DK))
    values = activated[:, 2 * HK :].reshape(piece_len, LOCAL_HEADS, DV)
    beta_gate = jax.nn.sigmoid(beta_logit[0].astype(jnp.float32)) * live_mask[:, None]
    decay_log = jnp.where(live_mask[:, None], log_decay[0], 0.0)
    inverse, beta_b, tables = block_tables(query_vec, key_vecs, beta_gate, decay_log, BLOCK)
    values_b = to_blocks(values, BLOCK)
    solved = solve_values(inverse, beta_b, values_b)
    zero_state = jnp.zeros((LOCAL_HEADS, DK, DV), jnp.float32)
    incoming = zero_state
    for section_index in range(seq_size - 1):
        ending, discarded = run_blocks(incoming, solved, tables)
        incoming = shifted(ending.astype(jnp.bfloat16), "seq", 1).astype(ending.dtype)
    ending, outputs = run_blocks(incoming, solved, tables)
    outputs = jnp.moveaxis(outputs, 1, 2).reshape(piece_len, LOCAL_HEADS, DV)
    is_last = seq_index == seq_size - 1
    state_term = jnp.where(is_last, ending, 0.0)
    targets = length - (CONV - 1) + jnp.arange(CONV - 1, dtype=jnp.int32)
    select = (position[None, :] == targets[:, None]).astype(jnp.bfloat16)
    edge_term = jnp.dot(select, tokens, preferred_element_type=jnp.float32)
    state_part, edge_part = (
        lax.psum_scatter(
            state_term.astype(jnp.bfloat16), "seq", scatter_dimension=0, tiled=True
        ).astype(jnp.float32),
        lax.psum_scatter(
            edge_term.astype(jnp.bfloat16), "seq", scatter_dimension=1, tiled=True
        ).astype(jnp.float32),
    )
    gate_values = gate_proj[0].astype(jnp.float32).reshape(piece_len, LOCAL_HEADS, DV)
    scaled = outputs * lax.rsqrt(jnp.mean(outputs * outputs, axis=-1, keepdims=True) + EPS_NORM)
    mixed_heads = (
        (scaled * norm_gain * jax.nn.silu(gate_values))
        .reshape(piece_len, LOCAL_HEADS * DV)
        .astype(jnp.bfloat16)
    )
    attended = jnp.dot(
        mixed_heads,
        lax.all_gather(out_weight, ("req", "seq"), axis=0, tiled=True),
        preferred_element_type=jnp.float32,
    )
    hidden_state = (residual[0].astype(jnp.float32) + attended).astype(jnp.bfloat16)
    stream = hidden_state.astype(jnp.float32)
    normed = (
        stream * lax.rsqrt(jnp.mean(stream * stream, axis=-1, keepdims=True) + EPS_NORM) * mlp_gain
    ).astype(jnp.bfloat16)
    gate_full, up_full = (
        lax.all_gather(w_gate, "req", axis=0, tiled=True),
        lax.all_gather(w_up, "req", axis=0, tiled=True),
    )
    down_full = lax.all_gather(w_down, "req", axis=1, tiled=True)
    shard_rows = lax.all_gather(normed, "seq", axis=0, tiled=True)
    gate_part = jnp.dot(shard_rows, gate_full, preferred_element_type=jnp.float32)
    upward = jnp.dot(shard_rows, up_full, preferred_element_type=jnp.float32)
    inner_units = (jax.nn.silu(gate_part) * upward).astype(jnp.bfloat16)
    summed = lax.psum_scatter(
        jnp.dot(inner_units, down_full, preferred_element_type=jnp.float32).astype(jnp.bfloat16),
        "seq",
        scatter_dimension=0,
        tiled=True,
    ).astype(jnp.float32)
    combined = stream + summed
    hidden_out = jnp.where(live_mask[:, None], combined, 0.0).astype(jnp.bfloat16)
    return (hidden_out[None], state_part[None], edge_part.astype(jnp.bfloat16)[None])


def solution(mesh):
    return jax.shard_map(
        local,
        mesh=mesh,
        in_specs=(
            P("req", "seq", None),
            P("req", "seq", None),
            P("req", "seq", None),
            P("req", "seq", None),
            P("req", "seq", None),
            P(),
            P(),
            P(),
            P(),
            P(("req", "seq"), None),
            P(),
            P("req", "seq"),
            P("req", "seq"),
            P("seq", "req"),
        ),
        out_specs=(P("req", "seq", None), P("req", "seq", None, None), P("req", None, "seq")),
        check_vma=False,
    )
```

profile of v0, /device:TPU:0, one launch (start us, length us, event | category | flops | bytes accessed | tf_op | source)
XLA Modules:
  0.0 511.9 jit_solution(8159952312244182873)
XLA Ops:
  25.7 80.0 %custom-call.3 = f32[8,2,1,64,64]{3,4,2,1,0:T(8,128)} custom-call(f32[8,2,1,64,64]{4,3,2,1,0:T(8,128)} %fusion.72), custom_call_target="InvertDiagBlocksLowerTriangular" | custom-call | tf_op jit(solution)/shard_map/triangular_solve | solution.py:47
  116.8 5.9 %collective-permute-start.1 = (bf16[8,128,256]{2,1,0:T(8,128)(2,1)}, bf16[8,128,256]{2,1,0:T(8,128)(2,1)}, u32[]{:S(2)}, u32[]{:S(2)}) collective-permute-start(bf16[8,128,256]{2,1,0:T(8,128)(2,1)} %convert_element_type.129), channel_id=1, source_target_pairs={{0,1},{1,2},{2,3},{3,4},{4,5},{5,6},{6,7},{8,9},{9,10},{10,11},{11... | collective-permute-start | bytes 1572872 | tf_op jit(solution)/shard_map/ppermute | solution.py:22
  124.5 4.2 while.83
  129.6 7.3 %collective-permute-start.2 = (bf16[8,128,256]{2,1,0:T(8,128)(2,1)}, bf16[8,128,256]{2,1,0:T(8,128)(2,1)}, u32[]{:S(2)}, u32[]{:S(2)}) collective-permute-start(bf16[8,128,256]{2,1,0:T(8,128)(2,1)} %convert_element_type.131), channel_id=1, source_target_pairs={{0,1},{1,2},{2,3},{3,4},{4,5},{5,6},{6,7},{8,9},{9,10},{10,11},{11... | collective-permute-start | bytes 1572872 | tf_op jit(solution)/shard_map/ppermute | solution.py:22
  139.1 4.2 while.84
  144.2 9.7 %collective-permute-start.3 = (bf16[8,128,256]{2,1,0:T(8,128)(2,1)}, bf16[8,128,256]{2,1,0:T(8,128)(2,1)}, u32[]{:S(2)}, u32[]{:S(2)}) collective-permute-start(bf16[8,128,256]{2,1,0:T(8,128)(2,1)} %convert_element_type.133), channel_id=1, source_target_pairs={{0,1},{1,2},{2,3},{3,4},{4,5},{5,6},{6,7},{8,9},{9,10},{10,11},{11... | collective-permute-start | bytes 1572872 | tf_op jit(solution)/shard_map/ppermute | solution.py:22
  156.1 4.2 while.85
  161.2 9.7 %collective-permute-start.4 = (bf16[8,128,256]{2,1,0:T(8,128)(2,1)}, bf16[8,128,256]{2,1,0:T(8,128)(2,1)}, u32[]{:S(2)}, u32[]{:S(2)}) collective-permute-start(bf16[8,128,256]{2,1,0:T(8,128)(2,1)} %convert_element_type.135), channel_id=1, source_target_pairs={{0,1},{1,2},{2,3},{3,4},{4,5},{5,6},{6,7},{8,9},{9,10},{10,11},{11... | collective-permute-start | bytes 1572872 | tf_op jit(solution)/shard_map/ppermute | solution.py:22
  173.2 4.2 while.86
  178.3 9.7 %collective-permute-start.5 = (bf16[8,128,256]{2,1,0:T(8,128)(2,1)}, bf16[8,128,256]{2,1,0:T(8,128)(2,1)}, u32[]{:S(2)}, u32[]{:S(2)}) collective-permute-start(bf16[8,128,256]{2,1,0:T(8,128)(2,1)} %convert_element_type.137), channel_id=1, source_target_pairs={{0,1},{1,2},{2,3},{3,4},{4,5},{5,6},{6,7},{8,9},{9,10},{10,11},{11... | collective-permute-start | bytes 1572872 | tf_op jit(solution)/shard_map/ppermute | solution.py:22
  195.2 9.7 %collective-permute-start.6 = (bf16[8,128,256]{2,1,0:T(8,128)(2,1)}, bf16[8,128,256]{2,1,0:T(8,128)(2,1)}, u32[]{:S(2)}, u32[]{:S(2)}) collective-permute-start(bf16[8,128,256]{2,1,0:T(8,128)(2,1)} %convert_element_type.139), channel_id=1, source_target_pairs={{0,1},{1,2},{2,3},{3,4},{4,5},{5,6},{6,7},{8,9},{9,10},{10,11},{11... | collective-permute-start | bytes 1572872 | tf_op jit(solution)/shard_map/ppermute | solution.py:22
  210.0 4.2 while.88
  214.2 6.3 %collective-permute-start.7 = (bf16[8,128,256]{2,1,0:T(8,128)(2,1)S(1)}, bf16[8,128,256]{2,1,0:T(8,128)(2,1)S(1)}, u32[]{:S(2)}, u32[]{:S(2)}) collective-permute-start(bf16[8,128,256]{2,1,0:T(8,128)(2,1)S(1)} %convert_element_type.141), channel_id=1, source_target_pairs={{0,1},{1,2},{2,3},{3,4},{4,5},{5,6},{6,7},{8,9},{9,10},{10,11},{11... | collective-permute-start | bytes 1572872 | tf_op jit(solution)/shard_map/ppermute | solution.py:22
  224.9 10.8 %while.89 = (s32[]{:T(128)}, f32[8,128,256]{2,1,0:T(8,128)S(1)}, f32[2,8,64,256]{3,2,1,0:T(8,128)}, f32[2,8]{1,0:T(2,128)S(1)}, f32[2,8,64,128]{3,2,1,0:T(8,128)...) while((s32[]{:T(128)}, f32[8,128,256]{2,1,0:T(8,128)S(1)}, ...), condition=%wide.region_20.21_spmd, body=%wide.region_19.20_spmd.sunk | while | flops 705429504 | bytes 19925256 | solution.py:87
  241.0 5.8 %multiply_reduce_fusion = (f32[128]{0:T(128)S(1)}, f32[128,2048]{1,0:T(8,128)S(1)}) fusion(bf16[2048,2048]{1,0:T(8,128)(2,1)} %all-gather.6.cloned.1.call-done, f32[128,2048]{1,0:T(8,128)} %bitcast.348, f32[128,2048]{1,0:T(8,128)} %bitcast.347, bf16[1,128,2048]{2,1,0:T(8,128)(2,1)} %param.31, f32[2048]{0:T(1024)S(1)} %bitcast.360, ...), kind=kOutput, calls=%fused_computation.125 | convolution fusion | flops 1077673856 | bytes 12591616 | tf_op jit(solution)/shard_map/dot_general | solution.py:160
  252.6 6.2 %all-gather.10.cloned.1.call-done = bf16[2048,704]{0,1:T(8,128)(2,1)} async-done(((bf16[128,704]{0,1:T(8,128)(2,1)}), bf16[2048,704]{0,1:T(8,128)(2,1)}) %all-gather.10.cloned.1.call-update) | async-done | bytes 2883600 | tf_op jit(solution)/shard_map/all_gather | solution.py:171
  258.8 34.0 %all-gather.8.cloned.1.call-done = bf16[1024,2048]{1,0:T(8,128)(2,1)} async-done(((bf16[128,2048]{1,0:T(8,128)(2,1)}), bf16[1024,2048]{1,0:T(8,128)(2,1)}) %all-gather.8.cloned.1.call-update) | async-done | bytes 4194320 | tf_op jit(solution)/shard_map/all_gather | solution.py:175
  292.8 7.8 %fusion.114 = f32[1024,704]{0,1:T(8,128)} fusion(bf16[1024,2048]{1,0:T(8,128)(2,1)} %all-gather.8.cloned.1.call-done, bf16[2048,704]{0,1:T(8,128)(2,1)} %all-gather.10.cloned.1.call-done), kind=kOutput, calls=%fused_computation.195 | convolution fusion | flops 2952790016 | bytes 9961472 | tf_op jit(solution)/shard_map/dot_general | solution.py:176
  300.7 44.4 %all-gather.12.cloned.1.call-done = bf16[2048,704]{0,1:T(8,128)(2,1)} async-done(((bf16[128,704]{0,1:T(8,128)(2,1)}), bf16[2048,704]{0,1:T(8,128)(2,1)}) %all-gather.12.cloned.1.call-update) | async-done | bytes 2883600 | tf_op jit(solution)/shard_map/all_gather | solution.py:172
  345.1 51.8 %all-gather.14.cloned.1.call-done = bf16[704,2048]{1,0:T(8,128)(2,1)} async-done(((bf16[704,128]{1,0:T(8,128)(2,1)}), bf16[704,2048]{1,0:T(8,128)(2,1)}) %all-gather.14.cloned.1.call-update) | async-done | bytes 2883600 | tf_op jit(solution)/shard_map/all_gather | solution.py:174
  396.9 12.0 %convolution_convert_fusion.1 = bf16[1024,2048]{1,0:T(8,128)(2,1)} fusion(bf16[704,2048]{1,0:T(8,128)(2,1)} %all-gather.14.cloned.1.call-done, f32[1024,704]{0,1:T(8,128)} %fusion.114, bf16[1024,2048]{1,0:T(8,128)(2,1)} %all-gather.8.cloned.1.call-done, bf16[2048,704]{0,1:T(8,128)(2,1)} %all-gather.12.cloned.1.call-done), kind=kOutput, calls=%fused_computation.94 | convolution fusion | flops 5912002560 | bytes 17039360 | tf_op jit(solution)/shard_map/dot_general | solution.py:180
  409.5 21.5 %reduce-scatter.10.cloned.1.call-done = bf16[512,3]{1,0:T(8,128)(2,1)} async-done(((bf16[4096,3]{1,0:T(8,128)(2,1)}), bf16[512,3]{1,0:T(8,128)(2,1)}) %reduce-scatter.10.cloned.1.call-update) | async-done | bytes 3088
  432.6 31.0 %reduce-scatter.8.cloned.1.call-done = bf16[1,128,256]{2,1,0:T(8,128)(2,1)} async-done(((bf16[8,128,256]{2,1,0:T(8,128)(2,1)}), bf16[1,128,256]{2,1,0:T(8,128)(2,1)}) %reduce-scatter.8.cloned.1.call-update) | async-done | bytes 65552 | tf_op jit(solution)/shard_map/reduce_scatter | solution.py:146
  465.1 37.8 %reduce-scatter.6.cloned.1.call-done = bf16[128,2048]{1,0:T(8,128)(2,1)} async-done(((bf16[1024,2048]{1,0:T(8,128)(2,1)}), bf16[128,2048]{1,0:T(8,128)(2,1)}) %reduce-scatter.6.cloned.1.call-update) | async-done | bytes 524304 | tf_op jit(solution)/shard_map/reduce_scatter | solution.py:179
  (201 shorter events, 113.3 us)
Async XLA Ops:
  7.2 198.2 %copy-start = (f32[256]{0:T(256)S(1)}, f32[256]{0:T(256)}, u32[]{:S(2)}) copy-start(f32[256]{0:T(256)} %param.38) | copy-start | bytes 3076
  7.2 233.8 %all-gather.6.cloned.1.call-start = ((), (), s32[]{:S(2)}) async-start(), calls=%async_computation.3 | async-start | bytes 8454144 | tf_op jit(solution)/shard_map/all_gather | solution.py:162
  8.1 9.1 %collective-permute-start = (bf16[3,4096]{1,0:T(4,128)(2,1)S(1)}, bf16[3,4096]{1,0:T(4,128)(2,1)S(1)}, u32[]{:S(2)}, u32[]{:S(2)}) collective-permute-start(bf16[3,4096]{1,0:T(4,128)(2,1)S(1)} %slice_bitcast_fusion.2), channel_id=1, source_target_pairs={{0,1},{1,2},{2,3},{3,4},{4,5},{5,6},{6,7},{8,9},{9,10},{10,11},{11... | collective-permute-start | bytes 73736 | tf_op jit(solution)/shard_map/ppermute | solution.py:22
  9.4 249.4 %all-gather.10.cloned.1.call-start = ((), (), s32[]{:S(2)}) async-start(), calls=%async_computation.5 | async-start | bytes 3063808 | tf_op jit(solution)/shard_map/all_gather | solution.py:171
  23.9 83.9 %copy-start.9 = (f32[8,2,64,128]{3,0,2,1:T(8,128)}, f32[8,2,64,128]{3,0,2,1:T(8,128)S(1)}, u32[]{:S(2)}) copy-start(f32[8,2,64,128]{3,0,2,1:T(8,128)S(1)} %get-tuple-element.663) | copy-start | bytes 1572868
  23.9 85.7 %slice-start = ((f32[128,4096]{1,0:T(8,128)}), f32[128,2048]{1,0:T(8,128)S(1)}, s32[]{:S(2)}) async-start(f32[128,4096]{1,0:T(8,128)} %copy-done.2), calls=%async_computation.11 | async-start | bytes 2097152 | tf_op jit(solution)/shard_map/slice | solution.py:127
  116.8 6.6 %collective-permute-start.1 = (bf16[8,128,256]{2,1,0:T(8,128)(2,1)}, bf16[8,128,256]{2,1,0:T(8,128)(2,1)}, u32[]{:S(2)}, u32[]{:S(2)}) collective-permute-start(bf16[8,128,256]{2,1,0:T(8,128)(2,1)} %convert_element_type.129), channel_id=1, source_target_pairs={{0,1},{1,2},{2,3},{3,4},{4,5},{5,6},{6,7},{8,9},{9,10},{10,11},{11... | collective-permute-start | bytes 1572872 | tf_op jit(solution)/shard_map/ppermute | solution.py:22
  129.6 8.3 %collective-permute-start.2 = (bf16[8,128,256]{2,1,0:T(8,128)(2,1)}, bf16[8,128,256]{2,1,0:T(8,128)(2,1)}, u32[]{:S(2)}, u32[]{:S(2)}) collective-permute-start(bf16[8,128,256]{2,1,0:T(8,128)(2,1)} %convert_element_type.131), channel_id=1, source_target_pairs={{0,1},{1,2},{2,3},{3,4},{4,5},{5,6},{6,7},{8,9},{9,10},{10,11},{11... | collective-permute-start | bytes 1572872 | tf_op jit(solution)/shard_map/ppermute | solution.py:22
  144.2 10.8 %collective-permute-start.3 = (bf16[8,128,256]{2,1,0:T(8,128)(2,1)}, bf16[8,128,256]{2,1,0:T(8,128)(2,1)}, u32[]{:S(2)}, u32[]{:S(2)}) collective-permute-start(bf16[8,128,256]{2,1,0:T(8,128)(2,1)} %convert_element_type.133), channel_id=1, source_target_pairs={{0,1},{1,2},{2,3},{3,4},{4,5},{5,6},{6,7},{8,9},{9,10},{10,11},{11... | collective-permute-start | bytes 1572872 | tf_op jit(solution)/shard_map/ppermute | solution.py:22
  161.2 10.8 %collective-permute-start.4 = (bf16[8,128,256]{2,1,0:T(8,128)(2,1)}, bf16[8,128,256]{2,1,0:T(8,128)(2,1)}, u32[]{:S(2)}, u32[]{:S(2)}) collective-permute-start(bf16[8,128,256]{2,1,0:T(8,128)(2,1)} %convert_element_type.135), channel_id=1, source_target_pairs={{0,1},{1,2},{2,3},{3,4},{4,5},{5,6},{6,7},{8,9},{9,10},{10,11},{11... | collective-permute-start | bytes 1572872 | tf_op jit(solution)/shard_map/ppermute | solution.py:22
  178.3 10.8 %collective-permute-start.5 = (bf16[8,128,256]{2,1,0:T(8,128)(2,1)}, bf16[8,128,256]{2,1,0:T(8,128)(2,1)}, u32[]{:S(2)}, u32[]{:S(2)}) collective-permute-start(bf16[8,128,256]{2,1,0:T(8,128)(2,1)} %convert_element_type.137), channel_id=1, source_target_pairs={{0,1},{1,2},{2,3},{3,4},{4,5},{5,6},{6,7},{8,9},{9,10},{10,11},{11... | collective-permute-start | bytes 1572872 | tf_op jit(solution)/shard_map/ppermute | solution.py:22
  195.2 13.6 %collective-permute-start.6 = (bf16[8,128,256]{2,1,0:T(8,128)(2,1)}, bf16[8,128,256]{2,1,0:T(8,128)(2,1)}, u32[]{:S(2)}, u32[]{:S(2)}) collective-permute-start(bf16[8,128,256]{2,1,0:T(8,128)(2,1)} %convert_element_type.139), channel_id=1, source_target_pairs={{0,1},{1,2},{2,3},{3,4},{4,5},{5,6},{6,7},{8,9},{9,10},{10,11},{11... | collective-permute-start | bytes 1572872 | tf_op jit(solution)/shard_map/ppermute | solution.py:22
  205.0 87.8 %all-gather.8.cloned.1.call-start = ((), (), s32[]{:S(2)}) async-start(), calls=%async_computation.4 | async-start | bytes 4718592 | tf_op jit(solution)/shard_map/all_gather | solution.py:175
  214.2 7.6 %copy-start.4 = (f32[16,8,8,128]{3,2,1,0:T(8,128)S(1)}, f32[16,8,8,128]{3,2,1,0:T(8,128)}, u32[]{:S(2)}) copy-start(f32[16,8,8,128]{3,2,1,0:T(8,128)} %copy.258) | copy-start | bytes 1572868
  214.2 8.8 %copy-start.10 = (f32[8,2,64,128]{3,0,2,1:T(8,128)S(1)}, f32[8,2,64,128]{3,0,2,1:T(8,128)}, u32[]{:S(2)}) copy-start(f32[8,2,64,128]{3,0,2,1:T(8,128)} %copy-done.9) | copy-start | bytes 1572868
  214.2 10.6 %collective-permute-start.7 = (bf16[8,128,256]{2,1,0:T(8,128)(2,1)S(1)}, bf16[8,128,256]{2,1,0:T(8,128)(2,1)S(1)}, u32[]{:S(2)}, u32[]{:S(2)}) collective-permute-start(bf16[8,128,256]{2,1,0:T(8,128)(2,1)S(1)} %convert_element_type.141), channel_id=1, source_target_pairs={{0,1},{1,2},{2,3},{3,4},{4,5},{5,6},{6,7},{8,9},{9,10},{10,11},{11... | collective-permute-start | bytes 1572872 | tf_op jit(solution)/shard_map/ppermute | solution.py:22
  241.0 5.8 %copy-start.11 = (f32[2048]{0:T(1024)S(1)}, f32[2048]{0:T(1024)}, u32[]{:S(2)}) copy-start(f32[2048]{0:T(1024)} %param.40) | copy-start | bytes 24580
  241.0 8.6 %copy-start.5 = (bf16[1,128,4096]{2,1,0:T(8,128)(2,1)S(1)}, bf16[1,128,4096]{2,1,0:T(8,128)(2,1)}, u32[]{:S(2)}) copy-start(bf16[1,128,4096]{2,1,0:T(8,128)(2,1)} %param.30) | copy-start | bytes 3145732
  247.8 97.3 %all-gather.12.cloned.1.call-start = ((), (), s32[]{:S(2)}) async-start(), calls=%async_computation.6 | async-start | bytes 3063808 | tf_op jit(solution)/shard_map/all_gather | solution.py:172
  248.4 148.5 %all-gather.14.cloned.1.call-start = ((), (), s32[]{:S(2)}) async-start(), calls=%async_computation.7 | async-start | bytes 3063808 | tf_op jit(solution)/shard_map/all_gather | solution.py:174
  249.0 182.0 %reduce-scatter.10.cloned.1.call-start = ((), (), s32[]{:S(2)}) async-start(), calls=%async_computation.10 | async-start | bytes 1179648
  251.3 212.2 %reduce-scatter.8.cloned.1.call-start = ((), (), s32[]{:S(2)}) async-start(), calls=%async_computation.9 | async-start | bytes 589824 | tf_op jit(solution)/shard_map/reduce_scatter | solution.py:146
  252.3 250.5 %reduce-scatter.6.cloned.1.call-start = ((), (), s32[]{:S(2)}) async-start(), calls=%async_computation.8 | async-start | bytes 4718592 | tf_op jit(solution)/shard_map/reduce_scatter | solution.py:179
  408.9 96.0 %copy-start.1 = (f32[256]{0:T(256)S(1)}, f32[256]{0:T(256)}, u32[]{:S(2)}) copy-start(f32[256]{0:T(256)} %param.38) | copy-start | bytes 3076
  (8 other events, 16.1 us)
Sparse Core Ops, SparseCore 0:
  11.0 74.0 all-gather.5
  205.1 53.6 all-gather.9
  261.1 31.6 all-gather.7
  294.8 50.2 all-gather.11
  347.0 49.8 all-gather.13
  399.2 31.8 reduce-scatter.9
  433.4 30.1 reduce-scatter.7
  466.0 36.8 reduce-scatter.5
where the time goes:
time: 521 us; the launch traced here: 512 us
  waiting for transfers between devices  233 us (45%)
  other arithmetic  114 us (22%)
  matrix products  71.7 us (14%)
  starting transfers between devices  60.5 us (12%)
  local copies, waits for them, and re-layouts  16.5 us (3%)
  between operations  15.4 us (3%)
    another operation x4, other arithmetic, block_tables(): lax.linalg.triangular_solve(identity + couple, identity, left_side=True,...  80.1 us
    ppermute x8, starting transfers between devices, shifted(): lax.ppermute(value, axis, [(source, source + steps) for source in range(i...  59.8 us
    all_gather x1, waiting for transfers between devices, local(): down_full = lax.all_gather(w_down, 'req', axis=1, tiled=True)  51.8 us
    all_gather x1, waiting for transfers between devices, local(): lax.all_gather(w_up, 'req', axis=0, tiled=True)  44.4 us
    reduce_scatter x1, waiting for transfers between devices, local(): lax.psum_scatter(jnp.dot(inner_units, down_full, preferred_element_type=j...  37.8 us
    all_gather x1, waiting for transfers between devices, local(): shard_rows = lax.all_gather(normed, 'seq', axis=0, tiled=True)  34 us
    reduce_scatter x1, waiting for transfers between devices, local(): lax.psum_scatter(state_term.astype(jnp.bfloat16), 'seq', scatter_dimensio...  31 us
    unnamed x9, waiting for transfers between devices  22.7 us
  transfers between devices with their start and end apart: 16, of which 12 were waited for; matrix products, arithmetic and copies ran while one was open for 39% of the time, Pallas kernels for 0%

commit v1 on v0

v1 whole, which is shorter than its diff:
```python
import functools

import jax
import jax.numpy as jnp
from jax import lax
from jax.experimental import pallas as pl
from jax.experimental.pallas import tpu as pltpu
from jax.sharding import PartitionSpec as P

MESH = pl.DeviceIdType.MESH
BF = jnp.bfloat16
F32 = jnp.float32

HEADS = 8
DK = 128
DV = 256
CONV = 4
HK = 1024
PIECE = 128
D = 2048
UNITS = 704
HALF = UNITS // 2
PAD = 16
EPS_NORM = 1e-05
EPS_UNIT = 1e-06


def dot(a, b):
    return jnp.dot(a, b, preferred_element_type=F32)


def dot_nt(a, b):
    return lax.dot_general(a, b, (((1,), (1,)), ((), ())), preferred_element_type=F32)


def parts(a):
    high = a.astype(BF)
    return high, (a - high.astype(F32)).astype(BF)


def left3(a):
    high, low = parts(a)
    return jnp.concatenate([high, high, low], axis=1)


def right3(a, axis=0):
    high, low = parts(a)
    return jnp.concatenate([high, low, high], axis=axis)


def silu(v):
    return v / (1.0 + jnp.exp(-v))


class Copies:
    def __init__(self, send, recv):
        self.send, self.recv, self.used, self.sent = send, recv, 0, []

    def take(self):
        self.used += 1
        return self.used - 1

    def start(self, index, view, device, own=None):
        src, dst = (own if own is not None else view()), view()
        copy = pltpu.make_async_remote_copy(
            src_ref=src,
            dst_ref=dst,
            send_sem=self.send.at[index],
            recv_sem=self.recv.at[index],
            device_id=device,
            device_id_type=MESH,
        )
        copy.start()
        self.sent.append((index, view, device))

    def arrived(self, index, dst, device):
        pltpu.make_async_remote_copy(
            src_ref=dst,
            dst_ref=dst,
            send_sem=self.send.at[index],
            recv_sem=self.recv.at[index],
            device_id=device,
            device_id_type=MESH,
        ).wait_recv()

    def drain(self):
        for index, view, device in self.sent:
            src = dst = view()
            pltpu.make_async_remote_copy(
                src_ref=src,
                dst_ref=dst,
                send_sem=self.send.at[index],
                recv_sem=self.recv.at[index],
                device_id=device,
                device_id_type=MESH,
            ).wait_send()
        self.sent = []


class Ring:
    def __init__(self, copies, me, plus, minus, items):
        self.copies, self.me, self.plus, self.minus = copies, me, plus, minus
        self.items = [(own, slot, half, [copies.take() for _ in range(4)]) for own, slot, half in items]
        self.left, self.right, self.far = (lax.rem(me + step, 4) for step in (3, 1, 2))

    def first(self):
        for own, slot, half, sems in self.items:
            view = functools.partial(slot, self.me)
            self.copies.start(sems[0], view, self.plus, own)
            self.copies.start(sems[1], view, self.minus, own)

    def second(self):
        for own, slot, half, sems in self.items:
            left, right = self.left, self.right
            self.copies.arrived(sems[0], slot(left), self.plus)
            self.copies.start(sems[2], functools.partial(half, left, 0), self.plus)
            self.copies.arrived(sems[1], slot(right), self.minus)
            self.copies.start(sems[3], functools.partial(half, right, 1), self.minus)

    def last(self):
        for own, slot, half, sems in self.items:
            far = self.far
            self.copies.arrived(sems[2], half(far, 0), self.plus)
            self.copies.arrived(sems[3], half(far, 1), self.minus)


def body(
    qkv, edge_in, gb_in, gate_in, res_in, out_w, w_gate, w_up, w_down,
    live, conv_w, norm_gain, mlp_gain,
    hidden, state_out, edge_out,
    kbuf, vbuf, qbuf, gbuf, ebuf,
    x3, kn_s, tv_s, tk_s, kd_s, a_s, qe_s, dec_s, w_s,
    obuf, mixed, gate, resid, stream,
    ow, wg, wu, wd, tok,
    hbuf, pown, psib, prec, s2, sn, r2, rn,
    send, recv, asend, arecv, bsend, brecv, local,
):
    req = lax.axis_index("req")
    seq = lax.axis_index("seq")
    y, x = lax.div(req, 4), lax.rem(req, 4)
    z, c = lax.div(seq, 2), lax.rem(seq, 2)
    other = 1 - c

    def up(v):
        return lax.rem(v + 1, 4)

    def down(v):
        return lax.rem(v + 3, 4)

    xu, xd, xf = up(x), down(x), lax.rem(x + 2, 4)
    yu, yd, yf = up(y), down(y), lax.rem(y + 2, 4)
    zu, zd, zf = up(z), down(z), lax.rem(z + 2, 4)
    xp, xm = (y * 4 + up(x), seq), (y * 4 + down(x), seq)
    yp, ym = (up(y) * 4 + x, seq), (down(y) * 4 + x, seq)
    zp, zm = (req, up(z) * 2 + c), (req, down(z) * 2 + c)
    sib = (req, z * 2 + other)

    barrier = pltpu.get_barrier_semaphore()
    for dev in (xp, xm, yp, ym):
        pl.semaphore_signal(barrier, inc=1, device_id=dev, device_id_type=MESH)
    for step in range(1, 8):
        pl.semaphore_signal(
            barrier, inc=1, device_id=(req, lax.rem(seq + step, 8)), device_id_type=MESH
        )

    def near(index, src, dst):
        return pltpu.make_async_copy(src, dst, local.at[index])

    qcol = pl.multiple_of(seq * DK, DK)
    kcol = pl.multiple_of(HK + seq * DK, DK)
    vcol = pl.multiple_of(2 * HK + seq * DV, DV)
    mine = pl.ds(pl.multiple_of(PAD + seq * PIECE, 16), PIECE)
    locals_ = [
        near(0, gb_in.at[seq], gbuf.at[seq]),
        near(1, qkv.at[:, pl.ds(kcol, DK)], kbuf.at[mine]),
        near(2, qkv.at[:, pl.ds(vcol, DV)], vbuf.at[mine]),
        near(3, qkv.at[:, pl.ds(qcol, DK)], qbuf.at[mine]),
        near(4, edge_in.at[seq], ebuf.at[seq]),
        near(5, gate_in, gate),
        near(6, res_in, resid),
        near(7, out_w, ow.at[y, x, z, c]),
        near(8, w_gate, wg.at[y, x]),
        near(9, w_up, wu.at[y, x]),
        near(10, w_down, wd.at[y, x]),
    ]
    for copy in locals_:
        copy.start()
    for buf in (kbuf, vbuf, qbuf):
        buf[0:PAD, :] = jnp.zeros((PAD, buf.shape[1]), BF)
    pl.semaphore_wait(barrier, 11)

    copies = Copies(send, recv)

    def cut(ref, first, size):
        return ref.at[pl.ds(first, size)]

    ring_oz = Ring(copies, z, zp, zm, [(
        out_w,
        lambda i: ow.at[y, x, i, c],
        lambda i, h: ow.at[y, x, i, c, :, h * 1024 : h * 1024 + 1024],
    )])
    ring_wax = Ring(copies, x, xp, xm, [
        (w_gate, lambda i: wg.at[y, i], lambda i, h: wg.at[y, i, h * 64 : h * 64 + 64]),
        (
            w_down.at[0:HALF],
            lambda i: wd.at[y, i, 0:HALF],
            lambda i, h: wd.at[y, i, h * 176 : h * 176 + 176],
        ),
    ])
    ring_wby = Ring(copies, y, yp, ym, [
        (w_up, lambda i: wu.at[i, x], lambda i, h: wu.at[i, x, h * 64 : h * 64 + 64]),
        (
            w_down.at[HALF:UNITS],
            lambda i: wd.at[i, x, HALF:UNITS],
            lambda i, h: wd.at[i, x, HALF + h * 176 : HALF + h * 176 + 176],
        ),
    ])
    ring_way = Ring(copies, y, yp, ym, [
        (None, lambda i: wg.at[i], lambda i, h: wg.at[i, 2 * h : 2 * h + 2]),
        (None, lambda i: wd.at[i, :, 0:HALF], lambda i, h: wd.at[i, 2 * h : 2 * h + 2, 0:HALF]),
    ])
    ring_wbx = Ring(copies, x, xp, xm, [
        (None, lambda i: wu.at[:, i], lambda i, h: wu.at[2 * h : 2 * h + 2, i]),
        (
            None,
            lambda i: wd.at[:, i, HALF:UNITS],
            lambda i, h: wd.at[2 * h : 2 * h + 2, i, HALF:UNITS],
        ),
    ])
    lo, hi = slice(0, 1024), slice(1024, 2048)
    ring_o1x = Ring(copies, x, xp, xm, [(
        None,
        lambda i: ow.at[y, i, :, c, :, lo],
        lambda i, h: ow.at[y, i, 2 * h : 2 * h + 2, c, :, lo],
    )])
    ring_o2y = Ring(copies, y, yp, ym, [(
        None,
        lambda i: ow.at[i, x, :, c, :, hi],
        lambda i, h: ow.at[i, x, 2 * h : 2 * h + 2, c, :, hi],
    )])
    ring_o1y = Ring(copies, y, yp, ym, [(
        None,
        lambda i: ow.at[i, :, :, c, :, lo],
        lambda i, h: ow.at[i, 2 * h : 2 * h + 2, :, c, :, lo],
    )])
    ring_o2x = Ring(copies, x, xp, xm, [(
        None,
        lambda i: ow.at[:, i, :, c, :, hi],
        lambda i, h: ow.at[2 * h : 2 * h + 2, i, :, c, :, hi],
    )])
    ring_tok = Ring(copies, z, zp, zm, [(
        None,
        lambda i: tok.at[i, c],
        lambda i, h: tok.at[i, c, h * 64 : h * 64 + 64],
    )])

    def exchange(kind, src, dst, dev, peer):
        return pltpu.make_async_remote_copy(
            src_ref=src, dst_ref=dst, send_sem=asend.at[kind, peer], recv_sem=arecv.at[kind, seq],
            device_id=dev, device_id_type=MESH,
        )

    def views(kind, head, piece):
        rows = pl.ds(pl.multiple_of(PAD + piece * PIECE, 16), PIECE)
        if kind == 0:
            return gb_in.at[head], gbuf.at[piece]
        if kind == 1:
            return qkv.at[:, pl.ds(pl.multiple_of(HK + head * DK, DK), DK)], kbuf.at[rows]
        if kind == 2:
            return qkv.at[:, pl.ds(pl.multiple_of(2 * HK + head * DV, DV), DV)], vbuf.at[rows]
        if kind == 3:
            return qkv.at[:, pl.ds(pl.multiple_of(head * DK, DK), DK)], qbuf.at[rows]
        return edge_in.at[head], ebuf.at[piece]

    order = (4, 3, 5, 2, 6, 7, 1)

    def spread(kind):
        for step in order:
            peer = lax.rem(seq + step, 8)
            src, dst = views(kind, peer, seq)
            exchange(kind, src, dst, (req, peer), peer).start()

    def piece_arrived(kind, piece):
        @pl.when(piece != seq)
        def _():
            src, dst = views(kind, seq, piece)
            pltpu.make_async_remote_copy(
                src_ref=dst, dst_ref=dst, send_sem=asend.at[kind, piece],
                recv_sem=arecv.at[kind, piece], device_id=(req, piece), device_id_type=MESH,
            ).wait_recv()

    ring_oz.first()
    spread(0)
    spread(1)
    ring_wax.first()
    ring_wby.first()
    ring_oz.second()
    spread(2)
    spread(3)
    spread(4)
    for index in range(4):
        locals_[index].wait()

    row = lax.broadcasted_iota(jnp.int32, (PIECE, PIECE), 0)
    col = lax.broadcasted_iota(jnp.int32, (PIECE, PIECE), 1)

    def convolve(buf, piece, taps):
        window = buf[pl.ds(pl.multiple_of(piece * PIECE, 16), PAD + PIECE), :].astype(F32)
        total = window[PAD:] * taps[CONV - 1 : CONV]
        for tap in range(CONV - 1):
            total = total + pltpu.roll(window, CONV - 1 - tap, 0)[PAD:] * taps[tap : tap + 1]
        return silu(total)

    def unit(v):
        return v * lax.rsqrt(jnp.sum(v * v, axis=-1, keepdims=True) + EPS_UNIT)

    def gates(piece):
        tile = gbuf[piece]
        log_row, beta_row = tile[0:1], tile[1:2]
        grown = jnp.sum(jnp.where(col <= row, log_row, 0.0), axis=1, keepdims=True)
        beta = jnp.sum(jnp.where(col == row, beta_row, 0.0), axis=1, keepdims=True)
        return log_row, grown, beta

    ktaps = conv_w[:, pl.ds(kcol, DK)]
    vtaps = conv_w[:, pl.ds(vcol, DV)]
    qtaps = conv_w[:, pl.ds(qcol, DK)]
    eye = jnp.where(row == col, 1.0, 0.0).astype(F32)

    GROUP = 4

    def invert(step, carry):
        pieces = [step * GROUP + j for j in range(GROUP)]
        for piece in pieces:
            piece_arrived(0, piece)
            piece_arrived(1, piece)
        couples, inverses = [], []
        for piece in pieces:
            key = unit(convolve(kbuf, piece, ktaps))
            kn_s[piece] = key
            log_row, grown, beta = gates(piece)
            log_col = jnp.sum(jnp.where(col == row, log_row, 0.0), axis=1, keepdims=True)
            along = jnp.sum(jnp.where(row <= col, log_col, 0.0), axis=0, keepdims=True)
            within = jnp.where(col <= row, jnp.exp(jnp.minimum(grown - along, 0.0)), 0.0)
            w_s[piece] = within
            inner = dot_nt(left3(key), right3(key, 1))
            couple = jnp.where(col < row, beta * within * inner, 0.0)
            couples.append(couple)
            inverses.append(eye - jnp.where((row // 2) == (col // 2), couple, 0.0))
        size = 2
        while size < PIECE:
            mask = ((row // (2 * size)) == (col // (2 * size))) & ((row // size) != (col // size))
            lows = [v.astype(BF) for v in inverses]
            mids = [
                dot(low, jnp.where(mask, couple, 0.0).astype(BF)).astype(BF)
                for low, couple in zip(lows, couples)
            ]
            inverses = [v - dot(mid, low) for v, mid, low in zip(inverses, mids, lows)]
            size *= 2
        rests = [
            eye - v - dot(left3(couple), right3(v)) for v, couple in zip(inverses, couples)
        ]
        for piece, v, rest in zip(pieces, inverses, rests):
            x3[piece] = left3(v + dot(v.astype(BF), rest.astype(BF)))

        @pl.when(step == 0)
        def _():
            ring_oz.last()
            locals_[7].wait()
            ring_o1x.first()
            ring_o2y.first()

        return carry

    lax.fori_loop(0, HEADS // GROUP, invert, 0)
    ring_wax.second()
    ring_wby.second()
    ring_o1x.second()
    ring_o2y.second()

    def prepare(step, carry):
        pieces = [step * 2 + j for j in range(2)]
        for piece in pieces:
            piece_arrived(2, piece)
            piece_arrived(3, piece)
        for piece in pieces:
            query = unit(convolve(qbuf, piece, qtaps)) * DK ** (-0.5)
            value = convolve(vbuf, piece, vtaps)
            key = kn_s[piece]
            log_row, grown, beta = gates(piece)
            whole = jnp.sum(log_row, axis=1, keepdims=True)
            growth = jnp.exp(grown)
            a_s[piece] = (w_s[piece] * dot_nt(left3(query), right3(key, 1))).astype(BF)
            qe_s[piece] = (growth * query).astype(BF)
            both = jnp.concatenate([beta * value, (beta * growth) * key], axis=1)
            solved = dot(x3[piece], right3(both))
            tv_s[piece] = solved[:, :DV]
            tk_s[piece] = left3(solved[:, DV:])
            kd_s[piece] = left3(jnp.transpose(jnp.exp(jnp.minimum(whole - grown, 0.0)) * key))
            dec_s[piece] = jnp.broadcast_to(jnp.exp(whole), (8, DV))

        return carry

    lax.fori_loop(0, HEADS // 2, prepare, 0)

    ring_o1x.last()
    ring_o2y.last()
    forwards = [copies.take() for _ in range(8)]

    def forward_o(first, index):
        copies.start(forwards[first], lambda: ow.at[index[0], :, :, c, :, lo], sib)
        copies.start(forwards[first + 1], lambda: ow.at[:, index[1], :, c, :, hi], sib)

    ring_o1y.first()
    ring_o2x.first()
    forward_o(0, (y, x))

    state_out[...] = jnp.zeros((DK, DV), F32)

    def back(piece):
        return pltpu.make_async_remote_copy(
            src_ref=obuf.at[piece], dst_ref=mixed.at[seq], send_sem=bsend.at[piece],
            recv_sem=brecv.at[seq], device_id=(req, piece), device_id_type=MESH,
        )

    def serial(piece, carry):
        running = state_out[...]
        corrected = tv_s[piece] - dot(tk_s[piece], right3(running))
        result = dot(qe_s[piece], running.astype(BF)) + dot(a_s[piece], corrected.astype(BF))
        state_out[...] = dec_s[piece][0:1] * running + dot(kd_s[piece], right3(corrected))
        scaled = result * lax.rsqrt(jnp.mean(result * result, axis=-1, keepdims=True) + EPS_NORM)

        @pl.when(piece == seq)
        def _():
            mixed[seq] = scaled.astype(BF)

        @pl.when(piece != seq)
        def _():
            obuf[piece] = scaled.astype(BF)
            back(piece).start()

        @pl.when(piece == 3)
        def _():
            ring_o1y.second()
            ring_o2x.second()
            forward_o(2, (yd, xd))
            forward_o(4, (yu, xu))

        return carry

    lax.fori_loop(0, HEADS, serial, 0)

    ring_wax.last()
    ring_wby.last()
    for index in (5, 6, 8, 9, 10):
        locals_[index].wait()
    ring_way.first()
    ring_wbx.first()

    ring_o1y.last()
    ring_o2x.last()
    forward_o(6, (yf, xf))

    for head in range(HEADS):
        @pl.when(head != seq)
        def _():
            pltpu.make_async_remote_copy(
                src_ref=mixed.at[head], dst_ref=mixed.at[head], send_sem=bsend.at[head],
                recv_sem=brecv.at[head], device_id=(req, head), device_id_type=MESH,
            ).wait_recv()

    gain = norm_gain[...]

    def gated(head, carry):
        columns = pl.ds(pl.multiple_of(head * DV, DV), DV)
        value = silu(gate[:, columns].astype(F32)) * gain
        mixed[head] = (mixed[head].astype(F32) * value).astype(BF)
        return carry

    lax.fori_loop(0, HEADS, gated, 0)

    for first, pair in ((0, (y, x)), (2, (yd, xd)), (4, (yu, xu)),
                        (6, (yf, xf))):
        copies.arrived(forwards[first], ow.at[pair[0], :, :, other, :, lo], sib)
        copies.arrived(forwards[first + 1], ow.at[:, pair[1], :, other, :, hi], sib)

    def project(tile, squares):
        columns = pl.ds(pl.multiple_of(tile * 256, 256), 256)
        attended = jnp.zeros((PIECE, 256), F32)
        for head in range(HEADS):
            rows = ow[head // 2, 2 * (head % 2) : 2 * (head % 2) + 2, :, :, :, columns]
            attended = attended + dot(mixed[head], rows.reshape(DV, 256))
        summed = (resid[:, columns].astype(F32) + attended).astype(BF)
        stream[:, columns] = summed
        wide = summed.astype(F32)
        return squares + jnp.sum(wide * wide, axis=-1, keepdims=True)

    squares = lax.fori_loop(0, D // 256, project, jnp.zeros((PIECE, 1), F32))
    scale = lax.rsqrt(squares * (1.0 / D) + EPS_NORM)
    tok[z, c] = (stream[...].astype(F32) * scale * mlp_gain[...]).astype(BF)

    tok_forward = [copies.take() for _ in range(4)]
    ring_tok.first()

    def forward_tok(index, zi):
        copies.start(tok_forward[index], lambda: tok.at[zi, c], sib)

    forward_tok(0, z)
    ring_tok.second()
    forward_tok(1, zd)
    forward_tok(2, zu)

    ring_way.second()
    ring_wbx.second()
    ring_tok.last()
    forward_tok(3, zf)
    for index, zi in ((0, z), (1, zd), (2, zu), (3, zf)):
        copies.arrived(tok_forward[index], tok.at[zi, other], sib)
    ring_way.last()
    ring_wbx.last()

    half_ids = [copies.take() for _ in range(4)]

    def cross(zi):
        return pltpu.make_async_remote_copy(
            src_ref=psib.at[zi], dst_ref=prec.at[zi], send_sem=bsend.at[8 + zi],
            recv_sem=brecv.at[8 + zi], device_id=sib, device_id_type=MESH,
        )

    def paired(zi):
        cross(zi).wait_recv()
        return pown[zi] + prec[zi].astype(F32)

    def far_sum():
        s2[...] = paired(zf).astype(BF)
        copies.start(half_ids[0], lambda: r2.at[0], zp, s2.at[0:64])
        copies.start(half_ids[1], lambda: r2.at[1], zm, s2.at[64:128])

    def next_sum(index):
        total = paired(zu if index == 0 else zd)
        copies.arrived(half_ids[index], r2.at[index], zp if index == 0 else zm)
        other_half = r2[index].astype(F32)
        if index == 0:
            sn[0, 0:64] = (total[0:64] + other_half).astype(BF)
            sn[0, 64:128] = total[64:128].astype(BF)
        else:
            sn[1, 0:64] = total[0:64].astype(BF)
            sn[1, 64:128] = (total[64:128] + other_half).astype(BF)
        copies.start(half_ids[2 + index], lambda: rn.at[index], zp if index == 0 else zm, sn.at[index])

    def ffn(step, carry):
        zi = (z + 10 - (step * (step + 1)) // 2) % 4
        tokens = jnp.concatenate([tok[zi, c], tok[zi, other]], axis=0)
        for first, width in ((0, 256), (256, 256), (512, 192)):
            gate_w = wg[:, :, :, first : first + width].reshape(D, width)
            up_w = wu[:, :, :, first : first + width].reshape(D, width)
            inner = silu(dot(tokens, gate_w)) * dot(tokens, up_w)
            hbuf[:, first : first + width] = inner.astype(BF)

        def lower(tile, carry):
            yi, xi = tile // 2, 2 * (tile % 2)
            rows = jnp.concatenate([wd[yi, xi], wd[yi, xi + 1]], axis=1)
            result = dot(hbuf[...], rows)
            columns = pl.ds(pl.multiple_of(tile * 256, 256), 256)
            pown[zi, :, columns] = result[:PIECE]
            psib[zi, :, columns] = result[PIECE:].astype(BF)
            return carry

        lax.fori_loop(0, D // 256, lower, 0)
        cross(zi).start()

        @pl.when(step == 1)
        def _():
            far_sum()

        @pl.when(step == 2)
        def _():
            next_sum(0)

        @pl.when(step == 3)
        def _():
            next_sum(1)

        return carry

    lax.fori_loop(0, 4, ffn, 0)

    total = stream[...].astype(F32) + paired(z)
    copies.arrived(half_ids[2], rn.at[0], zp)
    copies.arrived(half_ids[3], rn.at[1], zm)
    total = total + rn[0].astype(F32) + rn[1].astype(F32)
    hidden[...] = (total * live[...]).astype(BF)

    for piece in range(HEADS):
        piece_arrived(4, piece)
    locals_[4].wait()
    edges = ebuf[0].astype(F32)
    for piece in range(1, HEADS):
        edges = edges + ebuf[piece].astype(F32)
    edge_out[...] = edges.astype(BF)

    copies.drain()
    for kind in range(5):
        for step in order:
            peer = lax.rem(seq + step, 8)
            src, dst = views(kind, peer, seq)
            exchange(kind, src, dst, (req, peer), peer).wait_send()
    for step in range(1, 8):
        back(lax.rem(seq + step, 8)).wait_send()
    for zi in range(4):
        cross(zi).wait_send()


def layer(qkv, edge, gb, gate, residual, out_weight, w_gate, w_up, w_down, live, conv_weight, norm_gain, mlp_gain):
    hbm = pl.BlockSpec(memory_space=pl.ANY)
    vmem = pl.BlockSpec(memory_space=pltpu.VMEM)
    n_sems = 96
    scratch = [
        pltpu.VMEM((PAD + 1024, DK), BF),
        pltpu.VMEM((PAD + 1024, DV), BF),
        pltpu.VMEM((PAD + 1024, DK), BF),
        pltpu.VMEM((8, 8, 128), F32),
        pltpu.VMEM((8, 16, 512), BF),
        pltpu.VMEM((8, 128, 384), BF),
        pltpu.VMEM((8, 128, 128), F32),
        pltpu.VMEM((8, 128, 256), F32),
        pltpu.VMEM((8, 128, 384), BF),
        pltpu.VMEM((8, 128, 384), BF),
        pltpu.VMEM((8, 128, 128), BF),
        pltpu.VMEM((8, 128, 128), BF),
        pltpu.VMEM((8, 8, 256), F32),
        pltpu.VMEM((8, 128, 128), F32),
        pltpu.VMEM((8, 128, 256), BF),
        pltpu.VMEM((8, 128, 256), BF),
        pltpu.VMEM((128, 2048), BF),
        pltpu.VMEM((128, 2048), BF),
        pltpu.VMEM((128, 2048), BF),
        pltpu.VMEM((4, 4, 4, 2, 16, 2048), BF),
        pltpu.VMEM((4, 4, 128, UNITS), BF),
        pltpu.VMEM((4, 4, 128, UNITS), BF),
        pltpu.VMEM((4, 4, UNITS, 128), BF),
        pltpu.VMEM((4, 2, 128, 2048), BF),
        pltpu.VMEM((256, UNITS), BF),
        pltpu.VMEM((4, 128, 2048), F32),
        pltpu.VMEM((4, 128, 2048), BF),
        pltpu.VMEM((4, 128, 2048), BF),
        pltpu.VMEM((128, 2048), BF),
        pltpu.VMEM((2, 128, 2048), BF),
        pltpu.VMEM((2, 64, 2048), BF),
        pltpu.VMEM((2, 128, 2048), BF),
        pltpu.SemaphoreType.DMA((n_sems,)),
        pltpu.SemaphoreType.DMA((n_sems,)),
        pltpu.SemaphoreType.DMA((5, 8)),
        pltpu.SemaphoreType.DMA((5, 8)),
        pltpu.SemaphoreType.DMA((12,)),
        pltpu.SemaphoreType.DMA((12,)),
        pltpu.SemaphoreType.DMA((11,)),
    ]
    return pl.pallas_call(
        body,
        out_shape=(
            jax.ShapeDtypeStruct((PIECE, D), BF),
            jax.ShapeDtypeStruct((DK, DV), F32),
            jax.ShapeDtypeStruct((16, 512), BF),
        ),
        in_specs=[hbm] * 9 + [vmem] * 4,
        out_specs=(vmem, vmem, vmem),
        scratch_shapes=scratch,
        compiler_params=pltpu.CompilerParams(
            collective_id=0, has_side_effects=True, vmem_limit_bytes=64_000_000
        ),
        name="layer",
    )(qkv, edge, gb, gate, residual, out_weight, w_gate, w_up, w_down, live, conv_weight, norm_gain, mlp_gain)


def local_step(
    qkv_proj, gate_proj, residual, log_decay, beta_logit, lengths, slot_request, conv_weight,
    norm_gain, out_weight, mlp_gain, w_gate, w_up, w_down,
):
    seq_index = lax.axis_index("seq")
    req_index = lax.axis_index("req")
    ids = jnp.arange(slot_request.shape[0], dtype=jnp.int32)
    request = jnp.sum(jnp.where(ids == req_index, slot_request, 0))
    length = jnp.sum(jnp.where(ids == request, lengths, 0))
    position = seq_index * PIECE + jnp.arange(PIECE, dtype=jnp.int32)
    live = position < length
    beta = jax.nn.sigmoid(beta_logit[0].astype(F32)) * live[:, None]
    decay = jnp.where(live[:, None], log_decay[0], 0.0)
    gb = jnp.concatenate(
        [decay.T[:, None], beta.T[:, None], jnp.zeros((HEADS, 6, PIECE), F32)], axis=1
    )
    targets = length - (CONV - 1) + jnp.arange(16, dtype=jnp.int32)
    select = (position[None, :] == targets[:, None]) & (jnp.arange(16)[:, None] < CONV - 1)
    edge = jnp.dot(select.astype(BF), qkv_proj[0], preferred_element_type=F32).astype(BF)
    edge = edge.reshape(16, 8, 512).transpose(1, 0, 2)
    hidden, state, edges = layer(
        qkv_proj[0], edge, gb, gate_proj[0], residual[0], out_weight, w_gate, w_up, w_down,
        live.astype(F32)[:, None], conv_weight, norm_gain[None], mlp_gain[None],
    )
    return hidden[None], state[None, None], edges[None, : CONV - 1]


def solution(mesh):
    return jax.shard_map(
        local_step,
        mesh=mesh,
        in_specs=(
            P("req", "seq", None),
            P("req", "seq", None),
            P("req", "seq", None),
            P("req", "seq", None),
            P("req", "seq", None),
            P(),
            P(),
            P(),
            P(),
            P(("req", "seq"), None),
            P(),
            P("req", "seq"),
            P("req", "seq"),
            P("seq", "req"),
        ),
        out_specs=(P("req", "seq", None), P("req", "seq", None, None), P("req", None, "seq")),
        check_vma=False,
    )
```

time: 521 us -> 134 us (0.26); the launches traced: 512 us -> 134 us
  waiting for transfers between devices: 233 us -> 0 us
  Pallas kernels: 0 us -> 118 us
  other arithmetic: 114 us -> 4.57 us
  matrix products: 71.7 us -> 1.52 us
  starting transfers between devices: 60.5 us -> 0 us
  between operations: 15.4 us -> 1.36 us
  local copies, waits for them, and re-layouts: 16.5 us -> 8.01 us
    all_gather x5 -> x0, waiting for transfers between devices: 137 us -> none  [the longest x1 51.8 us: local(): down_full = lax.all_gather(w_down, 'req', axis=1, tiled=True)]
    pallas_call x0 -> x1, Pallas kernels: none -> 118 us  [layer(): pl.pallas_call(body, out_shape=(jax.ShapeDtypeStruct((PIECE, D), BF), jax...]
    another operation x5 -> x0, other arithmetic: 80.6 us -> none  [the longest x4 80.1 us: block_tables(): lax.linalg.triangular_solve(identity + couple, identity, left_side=True,...]
    reduce_scatter x2 -> x0, waiting for transfers between devices: 68.8 us -> none  [the longest x1 37.8 us: local(): lax.psum_scatter(jnp.dot(inner_units, down_full, preferred_element_type=j...]
    dot_general x44 -> x1, matrix products: 69.7 us -> 1.52 us  [local_step(): jnp.dot(select.astype(BF), qkv_proj[0], preferred_element_type=F32)]
    ppermute x8 -> x0, starting transfers between devices: 59.8 us -> none  [shifted(): lax.ppermute(value, axis, [(source, source + steps) for source in range(i...]
    unnamed x9 -> x0, waiting for transfers between devices: 22.7 us -> none
    convert_element_type x17 -> x2, other arithmetic: 14.8 us -> 1.95 us  [local_step(): beta = jax.nn.sigmoid(beta_logit[0].astype(F32)) * live[:, None]]
  transfers between devices with their start and end apart: 16 -> 0, of which waited for: 12 -> 0; matrix products, arithmetic and copies ran while one was open for 39% -> 0% of each run, Pallas kernels for 0% -> 0%
where the time goes in v1:
time: 134 us
  Pallas kernels  118 us (88%)
  local copies, waits for them, and re-layouts  8.01 us (6%)
  other arithmetic  4.57 us (3%)
  matrix products  1.52 us (1%)
  between operations  1.36 us (1%)
    pallas_call x1, Pallas kernels, layer(): pl.pallas_call(body, out_shape=(jax.ShapeDtypeStruct((PIECE, D), BF), jax...  118 us
    unnamed x18, local copies, waits for them, and re-layouts  5.96 us

profile of v1, /device:TPU:0, one launch (start us, length us, event | category | flops | bytes accessed | tf_op | source)
XLA Modules:
  0.0 133.8 jit_solution(1359047349705763839)
XLA Ops:
  0.6 0.0 copy-start.5
  0.6 0.6 copy-done.5
  1.3 0.0 copy-start.6
  1.3 0.6 fusion.6
  1.9 0.0 copy-done.6
  1.9 1.3 fusion.7
  3.9 0.1 pad.2.clone
  4.0 0.7 fusion.9
  4.7 0.0 copy-start.4
  4.7 0.0 copy-done.3
  4.7 0.7 copy-done.4
  5.3 0.7 maximum_maximum_fusion.gb_in
  6.0 1.3 fusion.live
  7.3 1.5 %convolution_convert_fusion = bf16[16,4096]{1,0:T(8,128)(2,1)S(1)} fusion(s32[128]{0:T(128)S(1)} %iota_add_fusion.1, s32[16]{0:T(128)S(1)} %iota_add_fusion, pred[16]{0:T(512)(128)(4,1)S(1)} %iota_compare_fusion, bf16[1,128,4096]{2,1,0:T(8,128)(2,1)} %param.14), kind=kOutput, calls=%fused_computation | convolution fusion | flops 16846848 | bytes 1180240 | tf_op jit(solution)/shard_map/dot_general | solution.py:693
  8.9 0.7 copy.28
  9.5 0.3 copy-done
  9.8 0.8 copy.24.w_gate
  10.7 0.1 copy-done.1
  10.8 0.8 copy.25.w_up
  11.6 118.4 %layer.1 = (bf16[128,2048]{1,0:T(8,128)(2,1)}, f32[128,256]{1,0:T(8,128)}, bf16[16,512]{1,0:T(8,128)(2,1)}) custom-call(bf16[128,4096]{1,0:T(8,128)(2,1)} %bitcast.28, bf16[8,16,512]{2,1,0:T(8,128)(2,1)} %bitcast.29, f32[8,8,128]{2,1,0:T(8,128)} %maximum_maximum_fusion.gb_in, bf16[128,2048]{1,0:T(8,128)(2,1)} %bitcast.32, bf16[128,2048]{1,0:T(8,128)(2,1)} %bitcast.33, ...), custom_call_target="tpu_custom_call" | custom-call | tf_op jit(solution)/shard_map/layer/pallas_call | solution.py:658
  129.9 1.3 slice_bitcast_fusion
  131.2 1.9 %copy.31 = bf16[1,128,2048]{2,1,0:T(8,128)(2,1)} copy(bf16[1,128,2048]{2,1,0:T(8,128)(2,1)} %bitcast.31) | data formatting | bytes 1048576
  133.2 0.0 copy-done.2
  133.2 0.7 copy.32
  (9 shorter events, 0.0 us)
Async XLA Ops:
  0.6 0.7 copy-start.5
  1.3 0.7 copy-start.6
  4.0 0.7 copy-start.3
  4.7 0.7 copy-start.4
  8.9 1.0 copy-start
  9.8 0.9 copy-start.1
  131.2 1.9 %copy-start.2 = (f32[128,256]{1,0:T(8,128)S(1)}, f32[128,256]{1,0:T(8,128)}, u32[]{:S(2)}) copy-start(f32[128,256]{1,0:T(8,128)} %get-tuple-element.7) | copy-start | bytes 393220

commit v2 on v1

--- a/solution.py
+++ b/solution.py
@@ -368,14 +368,20 @@
             locals_[7].wait()
             ring_o1x.first()
             ring_o2y.first()
+            ring_wax.second()
+            ring_wby.second()
 
         return carry
 
     lax.fori_loop(0, HEADS // GROUP, invert, 0)
-    ring_wax.second()
-    ring_wby.second()
     ring_o1x.second()
     ring_o2y.second()
+
+    forwards = [copies.take() for _ in range(8)]
+
+    def forward_o(first, index):
+        copies.start(forwards[first], lambda: ow.at[index[0], :, :, c, :, lo], sib)
+        copies.start(forwards[first + 1], lambda: ow.at[:, index[1], :, c, :, hi], sib)
 
     def prepare(step, carry):
         pieces = [step * 2 + j for j in range(2)]
@@ -398,21 +404,24 @@
             kd_s[piece] = left3(jnp.transpose(jnp.exp(jnp.minimum(whole - grown, 0.0)) * key))
             dec_s[piece] = jnp.broadcast_to(jnp.exp(whole), (8, DV))
 
+        @pl.when(step == 1)
+        def _():
+            ring_o1x.last()
+            ring_o2y.last()
+            ring_o1y.first()
+            ring_o2x.first()
+            forward_o(0, (y, x))
+
         return carry
 
     lax.fori_loop(0, HEADS // 2, prepare, 0)
 
-    ring_o1x.last()
-    ring_o2y.last()
-    forwards = [copies.take() for _ in range(8)]
-
-    def forward_o(first, index):
-        copies.start(forwards[first], lambda: ow.at[index[0], :, :, c, :, lo], sib)
-        copies.start(forwards[first + 1], lambda: ow.at[:, index[1], :, c, :, hi], sib)
-
-    ring_o1y.first()
-    ring_o2x.first()
-    forward_o(0, (y, x))
+    for index in (8, 9, 10):
+        locals_[index].wait()
+    ring_wax.last()
+    ring_wby.last()
+    ring_way.first()
+    ring_wbx.first()
 
     state_out[...] = jnp.zeros((DK, DV), F32)
 
@@ -449,12 +458,8 @@
 
     lax.fori_loop(0, HEADS, serial, 0)
 
-    ring_wax.last()
-    ring_wby.last()
-    for index in (5, 6, 8, 9, 10):
+    for index in (5, 6):
         locals_[index].wait()
-    ring_way.first()
-    ring_wbx.first()
 
     ring_o1y.last()
     ring_o2x.last()

time: 134 us -> 155 us (1.16)
  Pallas kernels: 118 us -> 139 us
    pallas_call x1, Pallas kernels: 118 us -> 139 us  [layer(): pl.pallas_call(body, out_shape=(jax.ShapeDtypeStruct((PIECE, D), BF), jax...]
where the time goes in v2:
time: 155 us
  Pallas kernels  139 us (90%)
  local copies, waits for them, and re-layouts  8.01 us (5%)
  other arithmetic  4.57 us (3%)
    pallas_call x1, Pallas kernels, layer(): pl.pallas_call(body, out_shape=(jax.ShapeDtypeStruct((PIECE, D), BF), jax...  139 us
    unnamed x18, local copies, waits for them, and re-layouts  5.96 us

profile of v2, /device:TPU:0, one launch (start us, length us, event | category | flops | bytes accessed | tf_op | source)
XLA Modules:
  0.0 154.7 jit_solution(2281781245110591074)
XLA Ops:
  0.6 0.0 copy-start.5
  0.6 0.6 copy-done.5
  1.3 0.0 copy-start.6
  1.3 0.6 fusion.6
  1.9 0.0 copy-done.6
  1.9 1.3 fusion.7
  3.9 0.1 pad.2.clone
  4.0 0.7 fusion.9
  4.7 0.0 copy-start.4
  4.7 0.0 copy-done.3
  4.7 0.7 copy-done.4
  5.3 0.7 maximum_maximum_fusion.gb_in
  6.0 1.3 fusion.live
  7.3 1.5 convolution_convert_fusion
  8.9 0.7 copy.28
  9.5 0.3 copy-done
  9.8 0.8 copy.24.w_gate
  10.7 0.1 copy-done.1
  10.8 0.8 copy.25.w_up
  11.6 139.2 %layer.1 = (bf16[128,2048]{1,0:T(8,128)(2,1)}, f32[128,256]{1,0:T(8,128)}, bf16[16,512]{1,0:T(8,128)(2,1)}) custom-call(bf16[128,4096]{1,0:T(8,128)(2,1)} %bitcast.28, bf16[8,16,512]{2,1,0:T(8,128)(2,1)} %bitcast.29, f32[8,8,128]{2,1,0:T(8,128)} %maximum_maximum_fusion.gb_in, bf16[128,2048]{1,0:T(8,128)(2,1)} %bitcast.32, bf16[128,2048]{1,0:T(8,128)(2,1)} %bitcast.33, ...), custom_call_target="tpu_custom_call" | custom-call | tf_op jit(solution)/shard_map/layer/pallas_call | solution.py:663
  150.8 1.3 slice_bitcast_fusion
  152.1 1.9 %copy.31 = bf16[1,128,2048]{2,1,0:T(8,128)(2,1)} copy(bf16[1,128,2048]{2,1,0:T(8,128)(2,1)} %bitcast.31) | data formatting | bytes 1048576
  154.0 0.0 copy-done.2
  154.0 0.7 copy.32
  (9 shorter events, 0.0 us)
Async XLA Ops:
  0.6 0.7 copy-start.5
  1.3 0.7 copy-start.6
  4.0 0.7 copy-start.3
  4.7 0.7 copy-start.4
  8.9 1.0 copy-start
  9.8 0.9 copy-start.1
  152.1 1.9 %copy-start.2 = (f32[128,256]{1,0:T(8,128)S(1)}, f32[128,256]{1,0:T(8,128)}, u32[]{:S(2)}) copy-start(f32[128,256]{1,0:T(8,128)} %get-tuple-element.7) | copy-start | bytes 393220
